TPU v7x, 32 devices: a whole 2x2x4 slice. The times are simulated.
32 devices in a mesh: dp: 8 (over z, x), seq: 4 (over y, core).
Axes of the slice: x: 2, y: 2, z: 4, core: 2. Of those that a mesh axis runs over, the one named last changes fastest.
Arguments:
- inputs: bfloat16 [8, 2048, 768], P('dp', 'seq'), may hold values from -2.5 to 2.5
- cotangent: bfloat16 [8, 2048, 768], P('dp', 'seq'), may hold values from -6 to 6
- qkv_weight: float32 [768, 2304], P('seq', 'dp'), may hold values from -0.21875 to 0.21875
- qkv_first: float32 [768, 2304], P('seq', 'dp'), may hold values from -128 to 128
- qkv_second: float32 [768, 2304], P('seq', 'dp'), may hold values from 491.52 to 4096
- out_weight: float32 [768, 768], P('seq', 'dp'), may hold values from -2.5 to 2.5
- out_first: float32 [768, 768], P('seq', 'dp'), may hold values from -13.57645 to 13.57645
- out_second: float32 [768, 768], P('seq', 'dp'), may hold values from 5.76 to 46.08
- fc_weight: float32 [768, 3072], P('seq', 'dp'), may hold values from -0.21875 to 0.21875
- fc_first: float32 [768, 3072], P('seq', 'dp'), may hold values from -46.08 to 46.08
- fc_second: float32 [768, 3072], P('seq', 'dp'), may hold values from 65.536 to 524.288
- proj_weight: float32 [3072, 768], P('seq', 'dp'), may hold values from -0.109375 to 0.109375
- proj_first: float32 [3072, 768], P('seq', 'dp'), may hold values from -97.28 to 97.28
- proj_second: float32 [3072, 768], P('seq', 'dp'), may hold values from 294.912 to 2359.296
- vectors: float32 [12, 768], P('seq', 'dp'), may hold values from -0.4 to 1.4, as said below
- vector_first: float32 [12, 768], P('seq', 'dp'), may hold values from -128 to 128
- vector_second: float32 [12, 768], P('seq', 'dp'), may hold values from 327.68 to 4096
Outputs:
- outputs: bfloat16 [8, 2048, 768], P('dp', 'seq')
- input_grad: bfloat16 [8, 2048, 768], P('dp', 'seq')
- qkv_first_new: float32 [768, 2304], P('seq', 'dp')
- qkv_second_new: float32 [768, 2304], P('seq', 'dp')
- qkv_updated: float32 [768, 2304], P('seq', 'dp')
- qkv_lowered: bfloat16 [768, 2304], P('seq', 'dp')
- out_first_new: float32 [768, 768], P('seq', 'dp')
- out_second_new: float32 [768, 768], P('seq', 'dp')
- out_updated: float32 [768, 768], P('seq', 'dp')
- out_lowered: bfloat16 [768, 768], P('seq', 'dp')
- fc_first_new: float32 [768, 3072], P('seq', 'dp')
- fc_second_new: float32 [768, 3072], P('seq', 'dp')
- fc_updated: float32 [768, 3072], P('seq', 'dp')
- fc_lowered: bfloat16 [768, 3072], P('seq', 'dp')
- proj_first_new: float32 [3072, 768], P('seq', 'dp')
- proj_second_new: float32 [3072, 768], P('seq', 'dp')
- proj_updated: float32 [3072, 768], P('seq', 'dp')
- proj_lowered: bfloat16 [3072, 768], P('seq', 'dp')
- vector_first_new: float32 [12, 768], P('seq', 'dp')
- vector_second_new: float32 [12, 768], P('seq', 'dp')
- vector_updated: float32 [12, 768], P('seq', 'dp')
- vector_lowered: bfloat16 [12, 768], P('seq', 'dp')
Inputs may be any that keep to these rules, and one draw needn't show every extreme that they name: `vectors`: rows 0 and 5 are LayerNorm gains near one, the other rows are biases of order a tenth.
All inputs are finite; a program needn't handle non-finite values.
Results may differ from a plain program's by a relative error of at most 0.018.
Values may be sent and summed in bfloat16 or wider, within the bound.
No kernel may reach another device: no remote copies, remote signals or barrier semaphores. Data moves between devices by JAX's collectives and lax.ppermute only.
A program may use at most 192 MiB of HBM per device.

v0:
```python
import jax
import jax.numpy as jnp
from jax import lax
from jax.sharding import PartitionSpec as P

D = 768
HEADS = 12
HEAD_DIM = 64
FF = 3072
DEPTH = 12
LEN = 2048
STEP = 10


beta_one = 0.5
beta_two = 0.5
matrix_decay = 0.1


def layer_norm(values, gain, shift):
    centre = values - jnp.mean(values, -1, keepdims=True)
    spread = jnp.mean(centre * centre, -1, keepdims=True)
    return centre * lax.rsqrt(spread + 1e-05) * gain + shift


def gelu_tanh(values):
    return jax.nn.gelu(values, approximate=True)


def adam_update(master, first, second, grad, rate, decay):
    first_new = beta_one * first + (1.0 - beta_one) * grad
    second_new = beta_two * second + (1.0 - beta_two) * grad * grad
    fix_one = 1.0 - beta_one**STEP
    fix_two = 1.0 - beta_two**STEP
    direction = first_new / fix_one / (jnp.sqrt(second_new / fix_two) + 1e-08)
    updated = master - rate * (direction + decay * master)
    return (first_new, second_new, updated, updated.astype(jnp.bfloat16))


def attend_forward(query_all, key_all, value_all):
    head_count, seq_len, head_width = query_all.shape
    block_len = min(512, seq_len)
    block_count = seq_len // block_len
    score_scale = head_width ** (-0.5)
    key_pos = jnp.arange(seq_len)[None, None, :]

    def one_block(block_index):
        block_start = block_index * block_len
        query_blk = lax.dynamic_slice_in_dim(query_all, block_start, block_len, 1)
        scores = (
            jnp.einsum("gqd,gkd->gqk", query_blk, key_all, preferred_element_type=jnp.float32)
            * score_scale
        )
        query_pos = block_start + jnp.arange(block_len)[None, :, None]
        scores = jnp.where(key_pos <= query_pos, scores, -1e30)
        row_max = jnp.max(scores, -1, keepdims=True)
        exponent = jnp.exp(scores - row_max)
        row_total = jnp.sum(exponent, -1, keepdims=True)
        attn_probs = (exponent / row_total).astype(jnp.bfloat16)
        block_out = jnp.einsum(
            "gqk,gkd->gqd", attn_probs, value_all, preferred_element_type=jnp.float32
        )
        return (block_out.astype(jnp.bfloat16), row_max + jnp.log(row_total))

    block_out, log_total = lax.map(one_block, jnp.arange(block_count))
    block_out = block_out.transpose(1, 0, 2, 3).reshape(head_count, seq_len, head_width)
    log_total = log_total.transpose(1, 0, 2, 3).reshape(head_count, seq_len, 1)
    return (block_out, log_total)


def attend_backward(query_all, key_all, value_all, grad_all, log_total):
    head_count, seq_len, head_width = query_all.shape
    block_len = min(512, seq_len)
    block_count = seq_len // block_len
    score_scale = head_width ** (-0.5)
    key_pos = jnp.arange(seq_len)[None, None, :]

    def one_block(carry, block_index):
        key_grad, value_grad = carry
        block_start = block_index * block_len
        query_blk = lax.dynamic_slice_in_dim(query_all, block_start, block_len, 1)
        grad_blk = lax.dynamic_slice_in_dim(grad_all, block_start, block_len, 1)
        total_blk = lax.dynamic_slice_in_dim(log_total, block_start, block_len, 1)
        scores = (
            jnp.einsum("gqd,gkd->gqk", query_blk, key_all, preferred_element_type=jnp.float32)
            * score_scale
        )
        query_pos = block_start + jnp.arange(block_len)[None, :, None]
        scores = jnp.where(key_pos <= query_pos, scores, -1e30)
        attn_probs = jnp.exp(scores - total_blk)
        grad_probs = jnp.einsum(
            "gqd,gkd->gqk", grad_blk, value_all, preferred_element_type=jnp.float32
        )
        inner = jnp.sum(attn_probs * grad_probs, -1, keepdims=True)
        grad_scores = (attn_probs * (grad_probs - inner)).astype(jnp.bfloat16)
        query_grad = (
            jnp.einsum("gqk,gkd->gqd", grad_scores, key_all, preferred_element_type=jnp.float32)
            * score_scale
        )
        key_grad = (
            key_grad
            + jnp.einsum("gqk,gqd->gkd", grad_scores, query_blk, preferred_element_type=jnp.float32)
            * score_scale
        )
        value_grad = value_grad + jnp.einsum(
            "gqk,gqd->gkd",
            attn_probs.astype(jnp.bfloat16),
            grad_blk,
            preferred_element_type=jnp.float32,
        )
        return ((key_grad, value_grad), query_grad)

    empty = jnp.zeros((head_count, seq_len, head_width), jnp.float32)
    (key_grad, value_grad), query_grad = lax.scan(
        one_block, (empty, empty), jnp.arange(block_count)
    )
    query_grad = query_grad.transpose(1, 0, 2, 3).reshape(head_count, seq_len, head_width)
    return jnp.stack([query_grad, key_grad, value_grad]).astype(jnp.bfloat16)


def token_sum(left, right):
    return jnp.einsum("ti,to->io", left, right, preferred_element_type=jnp.float32)


def back_product(grad_rows, weight):
    return jnp.einsum("to,io->ti", grad_rows, weight, preferred_element_type=jnp.float32)


def local(
    inputs,
    cotangent,
    qkv_weight,
    qkv_first,
    qkv_second,
    out_weight,
    out_first,
    out_second,
    fc_weight,
    fc_first,
    fc_second,
    proj_weight,
    proj_first,
    proj_second,
    vectors,
    vector_first,
    vector_second,
):
    branch = DEPTH ** (-0.5)
    seq_parts = lax.axis_size("seq")
    seq_count, part_len, features = inputs.shape
    tok_rows = seq_count * part_len
    seq_len = part_len * seq_parts
    head_groups = HEADS // seq_parts
    group_width = head_groups * HEAD_DIM
    low_qkv = qkv_weight.astype(jnp.bfloat16)
    low_out = out_weight.astype(jnp.bfloat16)
    low_fc = fc_weight.astype(jnp.bfloat16)
    low_proj = proj_weight.astype(jnp.bfloat16)
    low_vec = vectors.astype(jnp.bfloat16)
    wide_qkv, wide_out, wide_fc, wide_proj, wide_vec = (
        lax.all_gather(low_qkv, "dp", axis=1, tiled=True),
        lax.all_gather(low_out, "dp", axis=1, tiled=True),
        lax.all_gather(low_fc, "dp", axis=1, tiled=True),
        lax.all_gather(low_proj, "dp", axis=1, tiled=True),
        lax.all_gather(low_vec, "dp", axis=1, tiled=True),
    )
    w_qkv, w_out, w_fc, w_proj, w_vec = (
        lax.all_gather(wide_qkv, "seq", axis=0, tiled=True),
        lax.all_gather(wide_out, "seq", axis=0, tiled=True),
        lax.all_gather(wide_fc, "seq", axis=0, tiled=True),
        lax.all_gather(wide_proj, "seq", axis=0, tiled=True),
        lax.all_gather(wide_vec, "seq", axis=0, tiled=True),
    )
    vec_used = w_vec.astype(jnp.float32)
    tokens_in = inputs.astype(jnp.float32).reshape(tok_rows, features)
    h_one = layer_norm(tokens_in, vec_used[0], vec_used[1]).astype(jnp.bfloat16)
    qkv_bias = jnp.concatenate([vec_used[2], jnp.zeros_like(vec_used[2]), vec_used[3]])
    qkv_rows = (jnp.dot(h_one, w_qkv, preferred_element_type=jnp.float32) + qkv_bias).astype(
        jnp.bfloat16
    )
    outgoing = qkv_rows.reshape(seq_count, part_len, 3, seq_parts, group_width)
    arrived = lax.all_to_all(outgoing, "seq", split_axis=3, concat_axis=1, tiled=True)
    heads_all = arrived.reshape(seq_count, seq_len, 3, head_groups, HEAD_DIM).transpose(
        2, 0, 3, 1, 4
    )
    attn_heads, log_total = lax.map(
        lambda items: attend_forward(items[0], items[1], items[2]),
        (heads_all[0], heads_all[1], heads_all[2]),
    )
    leaving = attn_heads.transpose(0, 2, 1, 3).reshape(seq_count, seq_len, 1, group_width)
    returned = lax.all_to_all(leaving, "seq", split_axis=1, concat_axis=2, tiled=True)
    attn_rows = returned.reshape(tok_rows, features)
    attn_out = jnp.dot(attn_rows, w_out, preferred_element_type=jnp.float32) + vec_used[4]
    middle = tokens_in + branch * attn_out
    h_two = layer_norm(middle, vec_used[5], vec_used[6]).astype(jnp.bfloat16)
    hidden = jnp.dot(h_two, w_fc, preferred_element_type=jnp.float32) + vec_used[8:].reshape(-1)
    active = gelu_tanh(hidden).astype(jnp.bfloat16)
    mlp_out = jnp.dot(active, w_proj, preferred_element_type=jnp.float32) + vec_used[7]
    outputs = (middle + branch * mlp_out).astype(jnp.bfloat16).reshape(inputs.shape)
    back_qkv, back_out, back_fc, back_proj = (w_qkv, w_out, w_fc, w_proj)
    grad_out = cotangent.astype(jnp.float32).reshape(tok_rows, features)
    grad_mlp = (branch * grad_out).astype(jnp.bfloat16)
    grad_proj = token_sum(active, grad_mlp)
    grad_proj_bias = jnp.sum(grad_mlp.astype(jnp.float32), 0)
    grad_active = back_product(grad_mlp, back_proj)
    gelu_value, gelu_pull = jax.vjp(gelu_tanh, hidden)
    grad_hidden = gelu_pull(grad_active)[0].astype(jnp.bfloat16)
    grad_fc = token_sum(h_two, grad_hidden)
    grad_fc_bias = jnp.sum(grad_hidden.astype(jnp.float32), 0)
    grad_norm_two = back_product(grad_hidden, back_fc)
    norm_value, norm_pull = jax.vjp(layer_norm, middle, vec_used[5], vec_used[6])
    grad_mid_norm, grad_gain_two, grad_shift_two = norm_pull(grad_norm_two)
    grad_middle = grad_out + grad_mid_norm
    grad_attn_out = (branch * grad_middle).astype(jnp.bfloat16)
    grad_outproj = token_sum(attn_rows, grad_attn_out)
    grad_out_bias = jnp.sum(grad_attn_out.astype(jnp.float32), 0)
    grad_attn = back_product(grad_attn_out, back_out).astype(jnp.bfloat16)
    sending = grad_attn.reshape(seq_count, part_len, seq_parts, group_width)
    grad_arrived = lax.all_to_all(sending, "seq", split_axis=2, concat_axis=1, tiled=True)
    grad_heads = grad_arrived.reshape(seq_count, seq_len, head_groups, HEAD_DIM).transpose(
        0, 2, 1, 3
    )
    grad_qkv_heads = lax.map(
        lambda items: attend_backward(items[0], items[1], items[2], items[3], items[4]),
        (heads_all[0], heads_all[1], heads_all[2], grad_heads, log_total),
    )
    back_leaving = grad_qkv_heads.transpose(0, 3, 1, 2, 4).reshape(
        seq_count, seq_len, 3, 1, group_width
    )
    back_rows = lax.all_to_all(back_leaving, "seq", split_axis=1, concat_axis=3, tiled=True)
    grad_qkv = back_rows.reshape(tok_rows, 3 * features)
    grad_qkv_weight = token_sum(h_one, grad_qkv)
    qkv_sums = jnp.sum(grad_qkv.astype(jnp.float32), 0)
    grad_norm_one = back_product(grad_qkv, back_qkv)
    first_value, first_pull = jax.vjp(layer_norm, tokens_in, vec_used[0], vec_used[1])
    grad_in_norm, grad_gain_one, grad_shift_one = first_pull(grad_norm_one)
    input_grad = (grad_middle + grad_in_norm).astype(jnp.bfloat16).reshape(inputs.shape)
    grad_vec = jnp.concatenate(
        [
            jnp.stack(
                [
                    grad_gain_one,
                    grad_shift_one,
                    qkv_sums[:features],
                    qkv_sums[2 * features :],
                    grad_out_bias,
                    grad_gain_two,
                    grad_shift_two,
                    grad_proj_bias,
                ]
            ),
            grad_fc_bias.reshape(-1, features),
        ],
        0,
    )
    part_qkv, part_out, part_fc, part_proj, part_vec = (
        lax.psum_scatter(grad_qkv_weight, "dp", scatter_dimension=1, tiled=True),
        lax.psum_scatter(grad_outproj, "dp", scatter_dimension=1, tiled=True),
        lax.psum_scatter(grad_fc, "dp", scatter_dimension=1, tiled=True),
        lax.psum_scatter(grad_proj, "dp", scatter_dimension=1, tiled=True),
        lax.psum_scatter(grad_vec, "dp", scatter_dimension=1, tiled=True),
    )
    sum_qkv, sum_out, sum_fc, sum_proj, sum_vec = (
        lax.psum_scatter(
            part_qkv.astype(jnp.bfloat16), "seq", scatter_dimension=0, tiled=True
        ).astype(jnp.float32),
        lax.psum_scatter(
            part_out.astype(jnp.bfloat16), "seq", scatter_dimension=0, tiled=True
        ).astype(jnp.float32),
        lax.psum_scatter(
            part_fc.astype(jnp.bfloat16), "seq", scatter_dimension=0, tiled=True
        ).astype(jnp.float32),
        lax.psum_scatter(
            part_proj.astype(jnp.bfloat16), "seq", scatter_dimension=0, tiled=True
        ).astype(jnp.float32),
        lax.psum_scatter(
            part_vec.astype(jnp.bfloat16), "seq", scatter_dimension=0, tiled=True
        ).astype(jnp.float32),
    )
    qkv_new = adam_update(qkv_weight, qkv_first, qkv_second, sum_qkv, D ** (-0.5), matrix_decay)
    out_new = adam_update(
        out_weight, out_first, out_second, sum_out, max(1, 16 * D // LEN) ** (-0.5), matrix_decay
    )
    fc_new = adam_update(fc_weight, fc_first, fc_second, sum_fc, D ** (-0.5), matrix_decay)
    proj_new = adam_update(
        proj_weight, proj_first, proj_second, sum_proj, FF ** (-0.5), matrix_decay
    )
    vec_new = adam_update(vectors, vector_first, vector_second, sum_vec, 0.5, 0.0)
    return (
        outputs,
        input_grad,
        qkv_new[0],
        qkv_new[1],
        qkv_new[2],
        qkv_new[3],
        out_new[0],
        out_new[1],
        out_new[2],
        out_new[3],
        fc_new[0],
        fc_new[1],
        fc_new[2],
        fc_new[3],
        proj_new[0],
        proj_new[1],
        proj_new[2],
        proj_new[3],
        vec_new[0],
        vec_new[1],
        vec_new[2],
        vec_new[3],
    )


def solution(mesh):
    return jax.shard_map(
        local,
        mesh=mesh,
        in_specs=(
            P("dp", "seq", None),
            P("dp", "seq", None),
            P("seq", "dp"),
            P("seq", "dp"),
            P("seq", "dp"),
            P("seq", "dp"),
            P("seq", "dp"),
            P("seq", "dp"),
            P("seq", "dp"),
            P("seq", "dp"),
            P("seq", "dp"),
            P("seq", "dp"),
            P("seq", "dp"),
            P("seq", "dp"),
            P("seq", "dp"),
            P("seq", "dp"),
            P("seq", "dp"),
        ),
        out_specs=(
            P("dp", "seq", None),
            P("dp", "seq", None),
            P("seq", "dp"),
            P("seq", "dp"),
            P("seq", "dp"),
            P("seq", "dp"),
            P("seq", "dp"),
            P("seq", "dp"),
            P("seq", "dp"),
            P("seq", "dp"),
            P("seq", "dp"),
            P("seq", "dp"),
            P("seq", "dp"),
            P("seq", "dp"),
            P("seq", "dp"),
            P("seq", "dp"),
            P("seq", "dp"),
            P("seq", "dp"),
            P("seq", "dp"),
            P("seq", "dp"),
            P("seq", "dp"),
            P("seq", "dp"),
        ),
        check_vma=False,
    )
```

profile of v0, /device:TPU:0, one launch (start us, length us, event | category | flops | bytes accessed | tf_op | source)
XLA Modules:
  0.0 1290.6 jit_solution(14631618596200599561)
XLA Ops:
  9.1 35.4 %all_gather.32 = bf16[192,2304]{0,1:T(8,128)(2,1)S(1)} all-gather(bf16[192,288]{0,1:T(8,128)(2,1)S(1)} %convert_element_type.140), channel_id=1, replica_groups=mesh['dp'=8,'seq'=4] {'dp'}, dimensions={1}, use_global_device_ids=true | all-gather | bytes 995328 | tf_op jit(solution)/shard_map/all_gather | solution.py:161
  47.4 31.1 %all_gather.34 = bf16[192,768]{0,1:T(8,128)(2,1)S(1)} all-gather(bf16[192,96]{0,1:T(8,128)(2,1)S(1)} %convert_element_type.142), channel_id=1, replica_groups=mesh['dp'=8,'seq'=4] {'dp'}, dimensions={1}, use_global_device_ids=true | all-gather | bytes 331776 | tf_op jit(solution)/shard_map/all_gather | solution.py:162
  79.4 20.3 %all-gather = bf16[8,96,3]{1,2,0:T(4,128)(2,1)S(1)} all-gather(bf16[1,96,3]{1,2,0:T(4,128)(2,1)S(1)} %convert_bitcast_fusion.4), channel_id=1, replica_groups=mesh['dp'=8,'seq'=4] {'dp'}, dimensions={0}, use_global_device_ids=true | all-gather | bytes 5184 | tf_op jit(solution)/shard_map/all_gather | solution.py:165
  121.8 34.2 %all-to-all-done = bf16[1,512,3,4,192]{1,4,2,0,3:T(8,128)(2,1)S(1)} async-done(((bf16[1,512,3,4,192]{1,4,2,0,3:T(8,128)(2,1)}), bf16[1,512,3,4,192]{1,4,2,0,3:T(8,128)(2,1)S(1)}, u32[]{:S(2)}, u32[]{:S(2)}) %all-to-all-start) | async-done | bytes 2359328 | tf_op jit(solution)/shard_map/all_to_all | solution.py:182
  167.1 87.8 %while.46 = (s32[]{:T(128)}, bf16[4,3,512,64]{2,3,1,0:T(8,128)(2,1)}, f32[4,3,512,1]{2,1,3,0:T(4,128)S(1)}, s32[4]{0:T(128)S(1)}, bf16[3,2048,64]{1,2,0:T(8,128)...) while((s32[]{:T(128)}, ...), condition=%wide.region_5.6_spmd.clone, body=%wide.region_2.5_spmd.clone.sunk | while | flops 844200960 | bytes 43968700 | solution.py:65
  181.8 7.3 fusion.155
  203.8 7.3 fusion.155
  225.7 7.3 fusion.155
  247.6 7.3 fusion.155
  264.5 12.7 reduce.19
  283.2 11.5 all-to-all-done.1
  326.1 159.5 %reduce-scatter.24.cloned.1.call-done = f32[3072,96]{0,1:T(8,128)} async-done(((f32[3072,768]{0,1:T(8,128)}), f32[3072,96]{0,1:T(8,128)}) %reduce-scatter.24.cloned.1.call-update) | async-done | bytes 1179664 | tf_op jit(solution)/shard_map/reduce_scatter | solution.py:260
  487.9 21.9 %reduce-scatter.26.cloned.1.call-done = bf16[768,96]{0,1:T(8,128)(2,1)} async-done(((bf16[3072,96]{0,1:T(8,128)(2,1)}), bf16[768,96]{0,1:T(8,128)(2,1)}) %reduce-scatter.26.cloned.1.call-update) | async-done | bytes 147472 | tf_op jit(solution)/shard_map/reduce_scatter | solution.py:273
  512.4 41.2 %all-gather.17.cloned.1.call-done = bf16[768,768]{0,1:T(8,128)(2,1)} async-done(((bf16[768,96]{0,1:T(8,128)(2,1)}), bf16[768,768]{0,1:T(8,128)(2,1)}) %all-gather.17.cloned.1.call-update) | async-done | bytes 1179664 | tf_op jit(solution)/shard_map/all_gather | solution.py:164
  553.6 37.8 %all-gather.19.cloned.1.call-done = bf16[3072,768]{0,1:T(8,128)(2,1)} async-done(((bf16[768,768]{0,1:T(8,128)(2,1)}), bf16[3072,768]{0,1:T(8,128)(2,1)}) %all-gather.19.cloned.1.call-update) | async-done | bytes 4718608 | tf_op jit(solution)/shard_map/all_gather | solution.py:171
  591.5 10.6 convert_reduce_fusion
  622.1 7.8 all-to-all-done.2
  634.3 138.9 %while.47 = (s32[]{:T(128)}, f32[3,2048,64]{1,2,0:T(8,128)}, f32[3,2048,64]{1,2,0:T(8,128)}, bf16[4,3,512,64]{2,3,1,0:T(8,128)(2,1)}, s32[4]{0:T(128)S(1)}, /*in...) while((s32[]{:T(128)}, f32[3,2048,64]{1,2,0:T(8,128)}, ...), condition=%wide.region_12.13_spmd.clone, body=%wide.region_10.12_spmd.clone.sunk | while | flops 2063563776 | bytes 219593376 | solution.py:114
  639.9 7.4 multiply_reduce_fusion.5
  674.3 7.3 multiply_reduce_fusion.5
  709.1 7.3 multiply_reduce_fusion.5
  743.8 7.3 multiply_reduce_fusion.5
  782.4 53.9 %all_to_all.60 = bf16[1,2048,3,1,192]{4,2,3,0,1:T(4,128)(2,1)} all-to-all(bf16[1,2048,3,1,192]{4,2,3,0,1:T(4,128)(2,1)} %copy.188), channel_id=1, replica_groups=mesh['dp'=8,'seq'=4] {'seq'}, dimensions={1} | all-to-all | bytes 4718592 | tf_op jit(solution)/shard_map/all_to_all | solution.py:230
  836.2 7.2 copy.209
  851.4 9.0 fusion.93
  875.9 104.0 %reduce-scatter.16.cloned.1.call-done = f32[768,288]{0,1:T(8,128)} async-done(((f32[768,2304]{0,1:T(8,128)}), f32[768,288]{0,1:T(8,128)}) %reduce-scatter.16.cloned.1.call-update) | async-done | bytes 884752 | tf_op jit(solution)/shard_map/reduce_scatter | solution.py:257
  982.4 9.1 fusion.63
  991.5 155.0 %reduce-scatter.20.cloned.1.call-done = f32[768,384]{1,0:T(8,128)} async-done(((f32[768,3072]{1,0:T(8,128)}), f32[768,384]{1,0:T(8,128)}) %reduce-scatter.20.cloned.1.call-update) | async-done | bytes 1179664 | tf_op jit(solution)/shard_map/reduce_scatter | solution.py:259
  1151.8 58.6 %reduce-scatter.32.cloned.1.call-done = f32[96,12]{1,0:T(8,128)} async-done(((f32[768,12]{1,0:T(8,128)}), f32[96,12]{1,0:T(8,128)}) %reduce-scatter.32.cloned.1.call-update) | async-done | bytes 4624
  1218.3 14.1 %reduce-scatter.30.cloned.1.call-done = bf16[192,96]{1,0:T(8,128)(2,1)} async-done(((bf16[768,96]{1,0:T(8,128)(2,1)}), bf16[192,96]{1,0:T(8,128)(2,1)}) %reduce-scatter.30.cloned.1.call-update) | async-done | bytes 36880
  1237.3 19.7 %reduce-scatter.28.cloned.1.call-done = bf16[192,288]{1,0:T(8,128)(2,1)} async-done(((bf16[768,288]{1,0:T(8,128)(2,1)}), bf16[192,288]{1,0:T(8,128)(2,1)}) %reduce-scatter.28.cloned.1.call-update) | async-done | bytes 110608
  1262.7 18.9 %reduce-scatter.22.cloned.1.call-done = bf16[192,384]{1,0:T(8,128)(2,1)} async-done(((bf16[768,384]{1,0:T(8,128)(2,1)}), bf16[192,384]{1,0:T(8,128)(2,1)}) %reduce-scatter.22.cloned.1.call-update) | async-done | bytes 147472 | tf_op jit(solution)/shard_map/reduce_scatter | solution.py:270
  (451 shorter events, 335.9 us)
Async XLA Ops:
  7.2 99.6 %all-gather.9.cloned.1.call-start = ((), (), s32[]{:S(2)}) async-start(), calls=%async_computation.13 | async-start | bytes 4423680 | tf_op jit(solution)/shard_map/all_gather | solution.py:168
  44.5 61.1 %copy-start.9 = (bf16[1,512,768]{2,1,0:T(8,128)(2,1)S(1)}, bf16[1,512,768]{2,1,0:T(8,128)(2,1)}, u32[]{:S(2)}) copy-start(bf16[1,512,768]{2,1,0:T(8,128)(2,1)} %param.21) | copy-start | bytes 2359300
  45.8 75.4 %all-gather.13.cloned.1.call-start = ((), (), s32[]{:S(2)}) async-start(), calls=%async_computation.15 | async-start | bytes 1327104 | tf_op jit(solution)/shard_map/all_gather | solution.py:163
  46.6 261.9 %all-gather.11.cloned.1.call-start = ((), (), s32[]{:S(2)}) async-start(), calls=%async_computation.14 | async-start | bytes 1474560 | tf_op jit(solution)/shard_map/all_gather | solution.py:169
  117.5 38.4 %all-to-all-start = ((bf16[1,512,3,4,192]{1,4,2,0,3:T(8,128)(2,1)}), bf16[1,512,3,4,192]{1,4,2,0,3:T(8,128)(2,1)S(1)}, u32[]{:S(2)}, u32[]{:S(2)}) async-start(bf16[1,512,3,4,192]{1,4,2,0,3:T(8,128)(2,1)} %copy.176), calls=%async_computation | async-start | bytes 4718592 | tf_op jit(solution)/shard_map/all_to_all | solution.py:182
  121.2 191.3 %all-gather.15.cloned.1.call-start = ((), (), s32[]{:S(2)}) async-start(), calls=%async_computation.16 | async-start | bytes 5898240 | tf_op jit(solution)/shard_map/all_gather | solution.py:170
  279.6 15.1 %all-to-all-start.1 = ((bf16[4,2,49152]{2,1,0:T(2,128)(2,1)}), bf16[4,2,49152]{2,1,0:T(2,128)(2,1)S(1)}, u32[]{:S(2)}, u32[]{:S(2)}) async-start(bf16[4,2,49152]{2,1,0:T(2,128)(2,1)} %reshape.401), calls=%async_computation.1 | async-start | bytes 1572864 | tf_op jit(solution)/shard_map/all_to_all | solution.py:191
  283.1 202.6 %reduce-scatter.24.cloned.1.call-start = ((), (), s32[]{:S(2)}) async-start(), calls=%async_computation.23 | async-start | bytes 10616832 | tf_op jit(solution)/shard_map/reduce_scatter | solution.py:260
  283.1 308.3 %copy-start.55 = (f32[3072]{0:T(1024)}, f32[3072]{0:T(1024)S(1)}, u32[]{:S(2)}) copy-start(f32[3072]{0:T(1024)S(1)} %add.276) | copy-start | bytes 36868
  311.0 298.1 %copy-start.46 = (f32[512]{0:T(512)}, f32[512]{0:T(512)S(1)}, u32[]{:S(2)}) copy-start(f32[512]{0:T(512)S(1)} %broadcast_multiply_fusion) | copy-start | bytes 6148
  312.5 296.7 %copy-start.58 = (f32[512]{0:T(512)}, f32[512]{0:T(512)S(1)}, u32[]{:S(2)}) copy-start(f32[512]{0:T(512)S(1)} %fusion.89) | copy-start | bytes 6148
  326.1 183.7 %reduce-scatter.26.cloned.1.call-start = ((), (), s32[]{:S(2)}) async-start(), calls=%async_computation.24 | async-start | bytes 737280 | tf_op jit(solution)/shard_map/reduce_scatter | solution.py:273
  487.8 65.8 %all-gather.17.cloned.1.call-start = ((), (), s32[]{:S(2)}) async-start(), calls=%async_computation.17 | async-start | bytes 1327104 | tf_op jit(solution)/shard_map/all_gather | solution.py:164
  512.4 79.1 %all-gather.19.cloned.1.call-start = ((), (), s32[]{:S(2)}) async-start(), calls=%async_computation.18 | async-start | bytes 5898240 | tf_op jit(solution)/shard_map/all_gather | solution.py:171
  614.9 15.1 %all-to-all-start.2 = ((bf16[1,512,4,192]{1,3,0,2:T(8,128)(2,1)}), bf16[1,512,4,192]{1,3,0,2:T(8,128)(2,1)S(1)}, u32[]{:S(2)}, u32[]{:S(2)}) async-start(bf16[1,512,4,192]{1,3,0,2:T(8,128)(2,1)} %bitcast.202), calls=%async_computation.2 | async-start | bytes 1572864 | tf_op jit(solution)/shard_map/all_to_all | solution.py:219
  618.4 251.2 %reduce-scatter.18.cloned.1.call-start = ((), (), s32[]{:S(2)}) async-start(), calls=%async_computation.20 | async-start | bytes 2654208 | tf_op jit(solution)/shard_map/reduce_scatter | solution.py:258
  622.1 357.9 %reduce-scatter.16.cloned.1.call-start = ((), (), s32[]{:S(2)}) async-start(), calls=%async_computation.19 | async-start | bytes 7962624 | tf_op jit(solution)/shard_map/reduce_scatter | solution.py:257
  850.7 295.8 %reduce-scatter.20.cloned.1.call-start = ((), (), s32[]{:S(2)}) async-start(), calls=%async_computation.21 | async-start | bytes 10616832 | tf_op jit(solution)/shard_map/reduce_scatter | solution.py:259
  860.4 350.0 %reduce-scatter.32.cloned.1.call-start = ((), (), s32[]{:S(2)}) async-start(), calls=%async_computation.27 | async-start | bytes 442368
  869.5 362.9 %reduce-scatter.30.cloned.1.call-start = ((), (), s32[]{:S(2)}) async-start(), calls=%async_computation.26 | async-start | bytes 245760
  871.4 110.9 %copy-start.16 = (f32[512,768]{1,0:T(8,128)S(1)}, f32[512,768]{1,0:T(8,128)}, u32[]{:S(2)}) copy-start(f32[512,768]{1,0:T(8,128)} %copy-done.14) | copy-start | bytes 4718596
  871.4 110.9 %copy-start.56 = (f32[3072]{0:T(1024)S(1)}, f32[3072]{0:T(1024)}, u32[]{:S(2)}) copy-start(f32[3072]{0:T(1024)} %copy-done.55) | copy-start | bytes 36868
  871.4 110.9 %copy-start.61 = (f32[768]{0:T(1024)S(1)}, f32[768]{0:T(1024)}, u32[]{:S(2)}) copy-start(f32[768]{0:T(1024)} %get-tuple-element.359) | copy-start | bytes 9220
  871.4 385.6 %reduce-scatter.28.cloned.1.call-start = ((), (), s32[]{:S(2)}) async-start(), calls=%async_computation.25 | async-start | bytes 737280
  982.3 299.3 %reduce-scatter.22.cloned.1.call-start = ((), (), s32[]{:S(2)}) async-start(), calls=%async_computation.22 | async-start | bytes 737280 | tf_op jit(solution)/shard_map/reduce_scatter | solution.py:270
  991.4 157.3 %copy-start.8 = (f32[512,768]{1,0:T(8,128)S(1)}, f32[512,768]{1,0:T(8,128)}, u32[]{:S(2)}) copy-start(f32[512,768]{1,0:T(8,128)} %copy-done.7) | copy-start | bytes 4718596
  991.4 157.3 %copy-start.19 = (bf16[1,512,768]{2,1,0:T(8,128)(2,1)S(1)}, bf16[1,512,768]{2,1,0:T(8,128)(2,1)}, u32[]{:S(2)}) copy-start(bf16[1,512,768]{2,1,0:T(8,128)(2,1)} %param.22) | copy-start | bytes 2359300
  1148.7 84.6 %copy-start.29 = (f32[192,96]{0,1:T(8,128)S(1)}, f32[192,96]{0,1:T(8,128)}, u32[]{:S(2)}) copy-start(f32[192,96]{0,1:T(8,128)} %copy-done.28) | copy-start | bytes 221188
  1148.7 109.3 %copy-start.22 = (f32[192,288]{0,1:T(8,128)S(1)}, f32[192,288]{0,1:T(8,128)}, u32[]{:S(2)}) copy-start(f32[192,288]{0,1:T(8,128)} %copy-done.21) | copy-start | bytes 663556
  1235.8 45.8 %copy-start.27 = (f32[192,384]{1,0:T(8,128)S(1)}, f32[192,384]{1,0:T(8,128)}, u32[]{:S(2)}) copy-start(f32[192,384]{1,0:T(8,128)} %param.29) | copy-start | bytes 884740
  1235.8 45.8 %copy-start.34 = (f32[192,384]{1,0:T(8,128)S(1)}, f32[192,384]{1,0:T(8,128)}, u32[]{:S(2)}) copy-start(f32[192,384]{1,0:T(8,128)} %param.31) | copy-start | bytes 884740
  1235.8 45.8 %copy-start.35 = (f32[192,384]{1,0:T(8,128)S(1)}, f32[192,384]{1,0:T(8,128)}, u32[]{:S(2)}) copy-start(f32[192,384]{1,0:T(8,128)} %param.30) | copy-start | bytes 884740
  (104 other events, 538.4 us)
Sparse Core Ops, SparseCore 0:
  45.9 31.3 all-gather.8
  79.9 40.8 all-gather.12
  123.0 22.7 all-gather.10
  147.2 37.4 all-gather.14
  326.2 159.4 reduce-scatter.23
  488.6 21.1 reduce-scatter.25
  512.5 41.0 all-gather.16
  555.2 36.2 all-gather.18
  622.7 70.4 reduce-scatter.17
  850.8 129.1 reduce-scatter.15
  984.0 162.4 reduce-scatter.19
  1149.9 60.4 reduce-scatter.31
  1213.6 18.7 reduce-scatter.29
  1234.9 22.0 reduce-scatter.27
  1259.5 22.0 reduce-scatter.21
where the time goes:
time: 1300 us; the launch traced here: 1290 us
  waiting for transfers between devices  685 us (53%)
  matrix products  217 us (17%)
  blocking collectives  151 us (12%)
  local copies, waits for them, and re-layouts  102 us (8%)
  other arithmetic  100 us (8%)
  between operations  15.9 us (1%)
    reduce_scatter x1, waiting for transfers between devices, local(): lax.psum_scatter(grad_proj, 'dp', scatter_dimension=1, tiled=True)  160 us
    reduce_scatter x1, waiting for transfers between devices, local(): lax.psum_scatter(grad_fc, 'dp', scatter_dimension=1, tiled=True)  155 us
    reduce_scatter x1, waiting for transfers between devices, local(): lax.psum_scatter(grad_qkv_weight, 'dp', scatter_dimension=1, tiled=True)  104 us
    unnamed x18, waiting for transfers between devices  93.2 us
    all_to_all x1, blocking collectives, local(): lax.all_to_all(back_leaving, 'seq', split_axis=1, concat_axis=3, tiled=True)  53.9 us
    all_gather x1, waiting for transfers between devices, local(): lax.all_gather(low_proj, 'dp', axis=1, tiled=True)  41.2 us
    all_gather x1, waiting for transfers between devices, local(): lax.all_gather(wide_proj, 'seq', axis=0, tiled=True)  37.8 us
    all_gather x1, blocking collectives, local(): lax.all_gather(low_qkv, 'dp', axis=1, tiled=True)  35.4 us
  transfers between devices with their start and end apart: 18, of which 13 were waited for; matrix products, arithmetic and copies ran while one was open for 28% of the time, Pallas kernels for 0%

commit v1 on v0

v1 whole, which is shorter than its diff:
```python
import functools

import jax
import jax.numpy as jnp
from jax import lax
from jax.experimental import pallas as pl
from jax.experimental.pallas import tpu as pltpu
from jax.sharding import PartitionSpec as P

D = 768
HEADS = 12
HEAD_DIM = 64
FF = 3072
DEPTH = 12
LEN = 2048
STEP = 10
PARTS = 4
TOK = LEN // PARTS
OWN_HEADS = HEADS // PARTS
GROUP = OWN_HEADS * HEAD_DIM
ROWS = D // PARTS
FB = 8
FC = FF // FB
DB = D // FB
QB = 3 * D // FB
BRANCH = DEPTH ** (-0.5)
EPS = 1e-05

beta_one = 0.5
beta_two = 0.5
matrix_decay = 0.1

f32 = jnp.float32
bf16 = jnp.bfloat16

NN = (((1,), (0,)), ((), ()))
NT = (((1,), (1,)), ((), ()))
TN = (((0,), (0,)), ((), ()))


def dg(left, right, dims):
    return lax.dot_general(left, right, dims, preferred_element_type=f32)


def adam_update(master, first, second, grad, rate, decay):
    first_new = beta_one * first + (1.0 - beta_one) * grad
    second_new = beta_two * second + (1.0 - beta_two) * grad * grad
    fix_one = 1.0 - beta_one**STEP
    fix_two = 1.0 - beta_two**STEP
    direction = first_new / fix_one / (jnp.sqrt(second_new / fix_two) + 1e-08)
    updated = master - rate * (direction + decay * master)
    return (first_new, second_new, updated, updated.astype(bf16))


def swap(value, axis, k):
    n = lax.axis_size(axis)
    return lax.ppermute(value, axis, [(i, i ^ k) for i in range(n)])


def tree_swap(values, axis, k):
    return [swap(v, axis, k) for v in values]


def gather_dp(block):
    z = [block] + [swap(block, "dp", 2 * k) for k in (1, 2, 3)]
    z = jnp.stack(z)
    other = swap(z, "dp", 1)
    return jnp.stack([z, other], 1).reshape((8,) + block.shape)


def add_low(left, right):
    return (left.astype(f32) + right.astype(f32)).astype(bf16)


VM = pl.BlockSpec(memory_space=pltpu.VMEM)
SM = pl.BlockSpec(memory_space=pltpu.SMEM)


def vmem_call(kernel, args, outs, scratch, flops, name):
    moved = sum(a.size * a.dtype.itemsize for a in args)
    moved += sum(o.size * o.dtype.itemsize for o in outs)
    return pl.pallas_call(
        kernel,
        out_shape=tuple(outs),
        in_specs=[SM] + [VM] * (len(args) - 1),
        out_specs=tuple([VM] * len(outs)),
        scratch_shapes=list(scratch),
        compiler_params=pltpu.CompilerParams(vmem_limit_bytes=60 * 2**20),
        cost_estimate=pl.CostEstimate(flops=flops, bytes_accessed=moved, transcendentals=0),
        name=name,
    )(*args)


def shape(dims, dtype):
    return jax.ShapeDtypeStruct(dims, dtype)


def norm_parts(values):
    centre = values - jnp.mean(values, -1, keepdims=True)
    spread = jnp.mean(centre * centre, -1, keepdims=True)
    scale = lax.rsqrt(spread + EPS)
    return centre * scale, scale


def pick_kernel(place, wq, o0, o1, o2, o3, whole):
    b, s = place[0], place[1]
    for k in range(FB):
        whole[pl.ds(pl.multiple_of((b ^ k) * QB, 16), QB), :] = wq[k]
    for k, out in enumerate((o0, o1, o2, o3)):
        for p in range(3):
            at = pl.multiple_of(p * D + (s ^ k) * GROUP, 16)
            out[p * GROUP : (p + 1) * GROUP, :] = whole[pl.ds(at, GROUP), :]


def forward_kernel(
    place, x0, x1, x2, x3, w0, w1, w2, w3, vec, qbias, vbias,
    qkv, wt, at0, at1, at2, at3, lse, pieces, heads_out,
):
    s = place[1]
    for k, w in enumerate((w0, w1, w2, w3)):
        pieces[s ^ k] = w[...]
    for m in range(PARTS):
        wt[:, m * ROWS : (m + 1) * ROWS] = pieces[m]
    bias = jnp.concatenate([qbias[s], jnp.zeros((1, GROUP), f32), vbias[s]], 1)
    for k, x in enumerate((x0, x1, x2, x3)):
        rows = pl.ds(pl.multiple_of((s ^ k) * TOK, TOK), TOK)
        hat, _ = norm_parts(x[...].astype(f32))
        h = (hat * vec[0:1, :] + vec[1:2, :]).astype(bf16)
        r = (dg(h, wt[...], NT) + bias).astype(bf16)
        for i in range(3 * OWN_HEADS):
            part = r[:, i * HEAD_DIM : (i + 1) * HEAD_DIM]
            if i < OWN_HEADS:
                part = (part.astype(f32) * HEAD_DIM ** (-0.5)).astype(bf16)
            qkv[i, rows, :] = part

    def head(h, _):
        for i in range(PARTS):
            qi = qkv[h, i * TOK : (i + 1) * TOK, :]
            n = (i + 1) * TOK
            sc = dg(qkv[OWN_HEADS + h, 0:n, :], qi, NT)
            kp = lax.broadcasted_iota(jnp.int32, (TOK, TOK), 0)
            qp = lax.broadcasted_iota(jnp.int32, (TOK, TOK), 1)
            last = jnp.where(kp <= qp, sc[i * TOK :], -1e30)
            mx = jnp.max(last, 0, keepdims=True)
            if i:
                mx = jnp.maximum(mx, jnp.max(sc[: i * TOK], 0, keepdims=True))
            e_last = jnp.exp(last - mx)
            total = jnp.sum(e_last, 0, keepdims=True)
            e = e_last.astype(bf16)
            if i:
                e_first = jnp.exp(sc[: i * TOK] - mx)
                total = total + jnp.sum(e_first, 0, keepdims=True)
                e = jnp.concatenate([e_first.astype(bf16), e], 0)
            o = dg(qkv[2 * OWN_HEADS + h, 0:n, :], e, TN) / total
            heads_out[h, i * TOK : (i + 1) * TOK, :] = o.T.astype(bf16)
            lse[h, :, i * TOK : (i + 1) * TOK] = mx + jnp.log(total)
        return 0

    lax.fori_loop(0, OWN_HEADS, head, 0)
    for k, at in enumerate((at0, at1, at2, at3)):
        rows = pl.ds(pl.multiple_of((s ^ k) * TOK, TOK), TOK)
        for h in range(OWN_HEADS):
            at[:, h * HEAD_DIM : (h + 1) * HEAD_DIM] = heads_out[h, rows, :]


def backward_kernel(
    place, qkv, g0, g1, g2, g3, at0, at1, at2, at3, lse, wt, x0, x1, x2, x3, vec,
    dh0, dh1, dh2, dh3, gq0, gq1, gq2, gq3, gnorm, gbias,
    gout, delta, dheads, dkt, dvt, gsum, gpieces,
):
    s = place[1]
    for k, (g, at) in enumerate(zip((g0, g1, g2, g3), (at0, at1, at2, at3))):
        rows = pl.ds(pl.multiple_of((s ^ k) * TOK, TOK), TOK)
        gv = g[...]
        prod = gv.astype(f32) * at[...].astype(f32)
        for h in range(OWN_HEADS):
            lanes = slice(h * HEAD_DIM, (h + 1) * HEAD_DIM)
            gout[h, rows, :] = gv[:, lanes]
            delta[h, rows, :] = jnp.sum(prod[:, lanes], 1, keepdims=True)

    def head(h, _):
        for i in range(PARTS):
            cut = slice(i * TOK, (i + 1) * TOK)
            qi = qkv[h, cut, :]
            gi = gout[h, cut, :]
            di = delta[h, cut, :]
            li = lse[h, :, cut].T
            dq = jnp.zeros((TOK, HEAD_DIM), f32)
            for j in range(i + 1):
                keys = slice(j * TOK, (j + 1) * TOK)
                kj = qkv[OWN_HEADS + h, keys, :]
                vj = qkv[2 * OWN_HEADS + h, keys, :]
                sc = dg(qi, kj, NT)
                if j == i:
                    qp = lax.broadcasted_iota(jnp.int32, (TOK, TOK), 0)
                    kp = lax.broadcasted_iota(jnp.int32, (TOK, TOK), 1)
                    sc = jnp.where(kp <= qp, sc, -1e30)
                p = jnp.exp(sc - li)
                dp = dg(gi, vj, NT)
                ds = (p * (dp - di)).astype(bf16)
                dq = dq + dg(ds, kj, NN)
                dv = dg(gi, p.astype(bf16), TN)
                dk = dg(qi, ds, TN)
                if j == i:
                    dkt[:, keys] = dk
                    dvt[:, keys] = dv
                else:
                    dkt[:, keys] += dk
                    dvt[:, keys] += dv
            dheads[h, cut, :] = (dq * HEAD_DIM ** (-0.5)).astype(bf16)
        for j in range(PARTS):
            keys = slice(j * TOK, (j + 1) * TOK)
            dheads[OWN_HEADS + h, keys, :] = dkt[:, keys].T.astype(bf16)
            dheads[2 * OWN_HEADS + h, keys, :] = dvt[:, keys].T.astype(bf16)
        return 0

    lax.fori_loop(0, OWN_HEADS, head, 0)
    gsum[...] = jnp.zeros_like(gsum)
    gnorm[...] = jnp.zeros_like(gnorm)
    sums = jnp.zeros((1, 3 * GROUP), f32)
    for k, (x, dh) in enumerate(zip((x0, x1, x2, x3), (dh0, dh1, dh2, dh3))):
        rows = pl.ds(pl.multiple_of((s ^ k) * TOK, TOK), TOK)
        dqkv = jnp.concatenate([dheads[i, rows, :] for i in range(3 * OWN_HEADS)], 1)
        hat, _ = norm_parts(x[...].astype(f32))
        h = (hat * vec[0:1, :] + vec[1:2, :]).astype(bf16)
        gsum[...] += dg(dqkv, h, TN)
        sums = sums + jnp.sum(dqkv.astype(f32), 0, keepdims=True)
        part = dg(dqkv, wt[...], NN)
        dh[...] = part.astype(bf16)
        gnorm[0:1, :] += jnp.sum(part * hat, 0, keepdims=True)
        gnorm[1:2, :] += jnp.sum(part, 0, keepdims=True)
    gbias[...] = jnp.zeros_like(gbias)
    gbias[s] = sums
    for m in range(PARTS):
        gpieces[m] = gsum[:, m * ROWS : (m + 1) * ROWS].astype(bf16)
    for k, out in enumerate((gq0, gq1, gq2, gq3)):
        out[...] = gpieces[s ^ k]


def middle_kernel(
    place, a0, a1, a2, a3, x, cot, c0, c1, c2, c3, f0, f1, f2, f3, p0, p1, p2, p3, vec, fbias,
    out, act, du, h2, dm, da, dx1, d0, d1, d2, d3, gvec, gfb,
    wo, wf, wp, mid, macc, dacc,
):
    b, s = place[0], place[1]
    for k, c in enumerate((c0, c1, c2, c3)):
        for m in range(FB):
            wo[k, pl.ds(pl.multiple_of((b ^ m) * DB, 16), DB), :] = c[m]
    proj = dg(a0[...], wo[0], NT)
    for k, a in ((1, a1), (2, a2), (3, a3)):
        proj = proj + dg(a[...], wo[k], NT)
    x1 = x[...].astype(f32) + BRANCH * (proj + vec[4:5, :])
    mid[...] = x1
    hat, _ = norm_parts(x1)
    h2[...] = (hat * vec[5:6, :] + vec[6:7, :]).astype(bf16)
    low = (BRANCH * cot[...].astype(f32)).astype(bf16)
    dm[...] = low
    gvec[3:4, :] = jnp.sum(low.astype(f32), 0, keepdims=True)
    macc[...] = jnp.zeros_like(macc)
    dacc[...] = jnp.zeros_like(dacc)

    def chunk(t, _):
        k = t // 2
        j = t % 2
        f = 2 * (s ^ k) + j
        for m, w in enumerate((f0, f1, f2, f3)):
            wf[pl.ds(pl.multiple_of((s ^ m) * ROWS, 16), ROWS), :] = w[f ^ b]
        for q, w in enumerate((p0, p1, p2, p3)):

            @pl.when(k == q)
            def _():
                for m in range(FB):
                    wp[pl.ds(pl.multiple_of((b ^ m) * DB, 16), DB), :] = w[
                        m, :, pl.ds(pl.multiple_of(j * FC, FC), FC)
                    ]

        u = dg(h2[...], wf[...], NN) + fbias[f]
        coef = (2.0 / jnp.pi) ** 0.5
        th = jnp.tanh(coef * (u + 0.044715 * (u * u * u)))
        half = 0.5 * (1.0 + th)
        av = (u * half).astype(bf16)
        act[f] = av
        slope = half + 0.5 * u * (1.0 - th * th) * (coef * (1.0 + 3 * 0.044715 * (u * u)))
        dv = (dg(dm[...], wp[...], NN) * slope).astype(bf16)
        du[f] = dv
        gfb[f] = jnp.sum(dv.astype(f32), 0, keepdims=True)
        macc[...] += dg(av, wp[...], NT)
        dacc[...] += dg(dv, wf[...], NT)
        return 0

    lax.fori_loop(0, FB, chunk, 0)
    x1 = mid[...]
    out[...] = (x1 + BRANCH * (macc[...] + vec[7:8, :])).astype(bf16)
    hat, scale = norm_parts(x1)
    dh = dacc[...]
    gvec[1:2, :] = jnp.sum(dh * hat, 0, keepdims=True)
    gvec[2:3, :] = jnp.sum(dh, 0, keepdims=True)
    e = dh * vec[5:6, :]
    back = scale * (e - jnp.mean(e, -1, keepdims=True) - hat * jnp.mean(e * hat, -1, keepdims=True))
    dx = cot[...].astype(f32) + back
    dx1[...] = dx
    dlow = (BRANCH * dx).astype(bf16)
    da[...] = dlow
    gvec[0:1, :] = jnp.sum(dlow.astype(f32), 0, keepdims=True)
    for k, o in enumerate((d0, d1, d2, d3)):
        o[...] = dg(dlow, wo[k], NN).astype(bf16)


def grads_kernel(
    place, act, du, h2, dm, da, a0, a1, a2, a3,
    gf_send, gf_keep, gp_send, gp_keep, go_send, go_keep, wide, narrow,
):
    b, s = place[0], place[1]

    def by_block(m, _):
        wide[...] = dg(h2[...], du[b ^ m], TN).astype(bf16)
        for k in range(PARTS):
            out = gf_send if k % 2 else gf_keep
            out[k // 2, m] = wide[pl.ds(pl.multiple_of((s ^ k) * ROWS, 16), ROWS), :]
        return 0

    lax.fori_loop(0, FB, by_block, 0)
    for k in range(PARTS):
        out = gp_send if k % 2 else gp_keep
        for j in range(2):
            wide[...] = dg(dm[...], act[2 * (s ^ k) + j], TN).astype(bf16)
            for m in range(FB):
                out[k // 2, m, :, j * FC : (j + 1) * FC] = wide[
                    pl.ds(pl.multiple_of((b ^ m) * DB, 16), DB), :
                ]
    for k, a in enumerate((a0, a1, a2, a3)):
        out = go_send if k % 2 else go_keep
        narrow[...] = dg(da[...], a[...], TN).astype(bf16)
        for m in range(FB):
            out[k // 2, m] = narrow[pl.ds(pl.multiple_of((b ^ m) * DB, 16), DB), :]


def arrange_kernel(place, g0, g1, g2, g3, out, whole):
    b, s = place[0], place[1]
    for k, g in enumerate((g0, g1, g2, g3)):
        for p in range(3):
            at = pl.multiple_of(p * D + (s ^ k) * GROUP, 16)
            whole[pl.ds(at, GROUP), :] = g[p * GROUP : (p + 1) * GROUP, :]
    for m in range(FB):
        out[m] = whole[pl.ds(pl.multiple_of((b ^ m) * QB, 16), QB), :]


def last_kernel(place, dx1, own, other, x, vec, out):
    hat, scale = norm_parts(x[...].astype(f32))
    e = (own[...].astype(f32) + other[...].astype(f32)) * vec[0:1, :]
    back = scale * (e - jnp.mean(e, -1, keepdims=True) - hat * jnp.mean(e * hat, -1, keepdims=True))
    out[...] = (dx1[...] + back).astype(bf16)


def local(
    inputs, cotangent,
    qkv_weight, qkv_first, qkv_second,
    out_weight, out_first, out_second,
    fc_weight, fc_first, fc_second,
    proj_weight, proj_first, proj_second,
    vectors, vector_first, vector_second,
):
    dp = lax.axis_size("dp")
    by_pairs = dp == FB
    b = lax.axis_index("dp").astype(jnp.int32)
    s = lax.axis_index("seq").astype(jnp.int32)
    place = jnp.stack([b if by_pairs else jnp.zeros_like(b), s])
    split = dp // FB

    x = [inputs.reshape(TOK, D)]
    cot = cotangent.reshape(TOK, D)
    x.append(swap(x[0], "seq", 1))
    x.append(swap(x[0], "seq", 2))
    x.append(swap(x[2], "seq", 1))

    low_qkv = qkv_weight.astype(bf16).T
    low_fc = fc_weight.astype(bf16)
    low_proj = proj_weight.astype(bf16).T
    low_out = out_weight.astype(bf16).T
    if by_pairs:
        all_qkv = gather_dp(low_qkv)
        all_fc = gather_dp(low_fc)
        all_proj = gather_dp(low_proj)
        all_out = gather_dp(low_out)
    else:
        all_qkv = lax.all_gather(low_qkv, "dp").reshape(FB, QB, ROWS)
        all_fc = lax.all_gather(low_fc, "dp").reshape(FB, split, ROWS, FC // split)
        all_fc = all_fc.transpose(0, 2, 1, 3).reshape(FB, ROWS, FC)
        all_proj = lax.all_gather(low_proj, "dp").reshape(FB, DB, D)
        all_out = lax.all_gather(low_out, "dp").reshape(FB, DB, ROWS)
    vec_blocks = lax.all_gather(vectors.astype(bf16), ("dp", "seq"))
    vec = vec_blocks.reshape(dp, PARTS, 3, D // dp).transpose(1, 2, 0, 3).reshape(12, D).astype(f32)
    qbias = vec[2].reshape(PARTS, 1, GROUP)
    vbias = vec[3].reshape(PARTS, 1, GROUP)
    fbias = vec[8:].reshape(FB, 1, FC)

    picked = vmem_call(
        pick_kernel, [place, all_qkv], [shape((3 * GROUP, ROWS), bf16)] * PARTS,
        [pltpu.VMEM((3 * D, ROWS), bf16)], 0, "pick",
    )
    wq = [picked[0]] + [swap(picked[k], "seq", k) for k in (1, 2, 3)]

    def others(value):
        second = swap(value, "seq", 2)
        return [value, swap(value, "seq", 1), second, swap(second, "seq", 1)]

    wo = others(all_out)
    wf = others(all_fc)
    wp = others(all_proj)

    qkv, wt, at0, at1, at2, at3, lse = vmem_call(
        forward_kernel, [place, *x, *wq, vec, qbias, vbias],
        [shape((3 * OWN_HEADS, LEN, HEAD_DIM), bf16), shape((3 * GROUP, D), bf16)]
        + [shape((TOK, GROUP), bf16)] * PARTS + [shape((OWN_HEADS, 1, LEN), f32)],
        [pltpu.VMEM((PARTS, 3 * GROUP, ROWS), bf16), pltpu.VMEM((OWN_HEADS, LEN, HEAD_DIM), bf16)],
        6 * 10**9, "forward",
    )
    at = [at0, at1, at2, at3]
    rows = [at[0]] + [swap(at[k], "seq", k) for k in (1, 2, 3)]

    (out, act, du, h2, dm, da, dx1, d0, d1, d2, d3, gvec, gfb) = vmem_call(
        middle_kernel, [place, *rows, x[0], cot, *wo, *wf, *wp, vec, fbias],
        [shape((TOK, D), bf16), shape((FB, TOK, FC), bf16), shape((FB, TOK, FC), bf16)]
        + [shape((TOK, D), bf16)] * 3 + [shape((TOK, D), f32)] + [shape((TOK, GROUP), bf16)] * PARTS
        + [shape((4, D), f32), shape((FB, 1, FC), f32)],
        [pltpu.VMEM((PARTS, D, GROUP), bf16), pltpu.VMEM((D, FC), bf16), pltpu.VMEM((D, FC), bf16),
         pltpu.VMEM((TOK, D), f32), pltpu.VMEM((TOK, D), f32), pltpu.VMEM((TOK, D), f32)],
        12 * 10**9, "middle",
    )
    gout = [d0] + [swap(d, "seq", k) for k, d in ((1, d1), (2, d2), (3, d3))]

    grads = vmem_call(
        grads_kernel, [place, act, du, h2, dm, da, *rows],
        [shape((2, FB, ROWS, FC), bf16)] * 2 + [shape((2, FB, DB, D), bf16)] * 2
        + [shape((2, FB, DB, ROWS), bf16)] * 2,
        [pltpu.VMEM((D, FC), bf16), pltpu.VMEM((D, GROUP), bf16)], 6 * 10**9, "grads",
    )

    def reduce_dp(value, first):
        pair = value.reshape((4, 2) + value.shape[1:])
        got = swap(pair[:, 1], "dp", 1)
        part = add_low(pair[:, 0], got)
        total = part[0].astype(f32)
        for k in (1, 2, 3):
            total = total + swap(part[k], "dp", 2 * k).astype(f32)
        return total

    def reduce_all(send, keep, order):
        got = swap(send, "seq", 1)
        if order == "yx":
            other = add_low(keep[1], got[1])
            mine = add_low(keep[0], got[0])
            mine = add_low(mine, swap(other, "seq", 2))
            return reduce_dp(mine, None)
        pair_k = keep.reshape((2, 4, 2) + keep.shape[2:])
        pair_g = got.reshape((2, 4, 2) + keep.shape[2:])
        other = add_low(pair_k[:, :, 1], pair_g[:, :, 1])
        mine = add_low(pair_k[:, :, 0], pair_g[:, :, 0])
        mine = add_low(mine, swap(other, "dp", 1))
        part = add_low(mine[0], swap(mine[1], "seq", 2))
        total = part[0].astype(f32)
        for k in (1, 2, 3):
            total = total + swap(part[k], "dp", 2 * k).astype(f32)
        return total

    def reduce_plain(send, keep, kind):
        got = swap(send, "seq", 1)
        mine = add_low(keep[0], got[0])
        mine = add_low(mine, swap(add_low(keep[1], got[1]), "seq", 2))
        return scatter_plain(mine, kind)

    def scatter_plain(mine, kind):
        if kind == "fc":
            mine = mine.reshape(FB, ROWS, split, FC // split).transpose(0, 2, 1, 3)
            mine = mine.reshape(dp, ROWS, FC // split)
        else:
            mine = mine.reshape((dp, -1) + mine.shape[2:])
        return lax.psum_scatter(mine, "dp", scatter_dimension=0, tiled=False).astype(f32)

    if by_pairs:
        sum_fc = reduce_all(grads[0], grads[1], "yx")
        sum_proj = reduce_all(grads[2], grads[3], "xy").T
        sum_out = reduce_all(grads[4], grads[5], "yx").T
    else:
        sum_fc = reduce_plain(grads[0], grads[1], "fc")
        sum_proj = reduce_plain(grads[2], grads[3], "proj").T
        sum_out = reduce_plain(grads[4], grads[5], "out").T

    (dh0, dh1, dh2, dh3, gq0, gq1, gq2, gq3, gnorm, gbias) = vmem_call(
        backward_kernel, [place, qkv, *gout, *at, lse, wt, *x, vec],
        [shape((TOK, D), bf16)] * PARTS + [shape((3 * GROUP, ROWS), bf16)] * PARTS
        + [shape((2, D), f32), shape((PARTS, 1, 3 * GROUP), f32)],
        [pltpu.VMEM((OWN_HEADS, LEN, HEAD_DIM), bf16), pltpu.VMEM((OWN_HEADS, LEN, 1), f32),
         pltpu.VMEM((3 * OWN_HEADS, LEN, HEAD_DIM), bf16), pltpu.VMEM((HEAD_DIM, LEN), f32),
         pltpu.VMEM((HEAD_DIM, LEN), f32), pltpu.VMEM((3 * GROUP, D), f32),
         pltpu.VMEM((PARTS, 3 * GROUP, ROWS), bf16)],
        12 * 10**9, "backward",
    )
    gq = [gq0] + [swap(g, "seq", k) for k, g in ((1, gq1), (2, gq2), (3, gq3))]
    (blocks,) = vmem_call(
        arrange_kernel, [place, *gq], [shape((FB, QB, ROWS), bf16)],
        [pltpu.VMEM((3 * D, ROWS), bf16)], 0, "arrange",
    )
    sum_qkv = (reduce_dp(blocks, None) if by_pairs else scatter_plain(blocks, "qkv")).T

    own = add_low(dh0, swap(dh1, "seq", 1))
    other = swap(add_low(dh2, swap(dh3, "seq", 1)), "seq", 2)
    (input_grad,) = vmem_call(
        last_kernel, [place, dx1, own, other, x[0], vec], [shape((TOK, D), bf16)], [], 0, "last"
    )

    gb = gbias.reshape(PARTS, 3, GROUP)
    grad_vec = jnp.concatenate(
        [
            gnorm,
            gb[:, 0].reshape(1, D),
            gb[:, 2].reshape(1, D),
            gvec,
            gfb.reshape(4, D),
        ],
        0,
    )
    total_vec = lax.psum(grad_vec, ("dp", "seq"))
    width = D // dp
    sum_vec = lax.dynamic_slice(total_vec, (s * 3, b * width), (3, width))

    qkv_new = adam_update(qkv_weight, qkv_first, qkv_second, sum_qkv, D ** (-0.5), matrix_decay)
    out_new = adam_update(
        out_weight, out_first, out_second, sum_out, max(1, 16 * D // LEN) ** (-0.5), matrix_decay
    )
    fc_new = adam_update(fc_weight, fc_first, fc_second, sum_fc, D ** (-0.5), matrix_decay)
    proj_new = adam_update(
        proj_weight, proj_first, proj_second, sum_proj, FF ** (-0.5), matrix_decay
    )
    vec_new = adam_update(vectors, vector_first, vector_second, sum_vec, 0.5, 0.0)
    return (
        out.reshape(inputs.shape),
        input_grad.reshape(inputs.shape),
        *qkv_new,
        *out_new,
        *fc_new,
        *proj_new,
        *vec_new,
    )


def solution(mesh):
    rows = P("dp", "seq", None)
    block = P("seq", "dp")
    return jax.shard_map(
        local,
        mesh=mesh,
        in_specs=(rows, rows) + (block,) * 15,
        out_specs=(rows, rows) + (block,) * 20,
        check_vma=False,
    )
```

time: 1300 us -> 474 us (0.36)
  waiting for transfers between devices: 685 us -> 158 us
  matrix products: 217 us -> 0 us
  Pallas kernels: 0 us -> 107 us
  local copies, waits for them, and re-layouts: 102 us -> 18.1 us
  other arithmetic: 100 us -> 28.2 us
  blocking collectives: 151 us -> 83.1 us
  starting transfers between devices: 11.5 us -> 70.8 us
  between operations: 15.9 us -> 1.71 us
    reduce_scatter x6 -> x0, waiting for transfers between devices: 459 us -> none  [the longest x1 160 us: local(): lax.psum_scatter(grad_proj, 'dp', scatter_dimension=1, tiled=True)]
    dot_general x40 -> x0, matrix products: 217 us -> none  [the longest x8 31.2 us: one_block(): jnp.einsum('gqd,gkd->gqk', query_blk, key_all, preferred_element_type=jnp...]
    ppermute x0 -> x65, waiting for transfers between devices: none -> 158 us  [swap(): return lax.ppermute(value, axis, [(i, i ^ k) for i in range(n)])]
    pallas_call x0 -> x7, Pallas kernels: none -> 107 us  [vmem_call(): pl.pallas_call(kernel, out_shape=tuple(outs), in_specs=[SM] + [VM] * (len...]
    unnamed x18 -> x0, waiting for transfers between devices: 93.2 us -> none
    all_gather x6 -> x0, waiting for transfers between devices: 79.1 us -> none  [the longest x1 41.2 us: local(): lax.all_gather(low_proj, 'dp', axis=1, tiled=True)]
    ppermute x0 -> x65, starting transfers between devices: none -> 70.8 us  [swap(): return lax.ppermute(value, axis, [(i, i ^ k) for i in range(n)])]
    all_to_all x1 -> x0, blocking collectives: 53.9 us -> none  [local(): lax.all_to_all(back_leaving, 'seq', split_axis=1, concat_axis=3, tiled=True)]
  transfers between devices with their start and end apart: 18 -> 65, of which waited for: 13 -> 21; matrix products, arithmetic and copies ran while one was open for 28% -> 8% of each run, Pallas kernels for 0% -> 17%
where the time goes in v1:
time: 474 us; the launch traced here: 467 us
  waiting for transfers between devices  158 us (33%)
  Pallas kernels  107 us (23%)
  blocking collectives  83.1 us (18%)
  starting transfers between devices  70.8 us (15%)
  other arithmetic  28.2 us (6%)
  local copies, waits for them, and re-layouts  18.1 us (4%)
    ppermute x65, waiting for transfers between devices, swap(): return lax.ppermute(value, axis, [(i, i ^ k) for i in range(n)])  158 us
    pallas_call x7, Pallas kernels, vmem_call(): pl.pallas_call(kernel, out_shape=tuple(outs), in_specs=[SM] + [VM] * (len...  107 us
    ppermute x65, starting transfers between devices, swap(): return lax.ppermute(value, axis, [(i, i ^ k) for i in range(n)])  70.8 us
    psum x1, blocking collectives, local(): total_vec = lax.psum(grad_vec, ('dp', 'seq'))  43.9 us
    all_gather x1, blocking collectives, local(): vec_blocks = lax.all_gather(vectors.astype(bf16), ('dp', 'seq'))  39.2 us
    convert_element_type x12, other arithmetic, add_low(): return (left.astype(f32) + right.astype(f32)).astype(bf16)  13.1 us
  transfers between devices with their start and end apart: 65, of which 21 were waited for; matrix products, arithmetic and copies ran while one was open for 8% of the time, Pallas kernels for 17%

profile of v1, /device:TPU:0, one launch (start us, length us, event | category | flops | bytes accessed | tf_op | source)
XLA Modules:
  0.0 466.6 jit_solution(17165910056592459070)
XLA Ops:
  1.7 4.1 collective-permute-start.21
  10.4 2.5 collective-permute-start.27
  14.5 7.3 %collective-permute-start.29 = (bf16[96,768]{1,0:T(8,128)(2,1)S(1)}, bf16[96,768]{1,0:T(8,128)(2,1)S(1)}, u32[]{:S(2)}, u32[]{:S(2)}) collective-permute-start(bf16[96,768]{1,0:T(8,128)(2,1)S(1)} %get-tuple-element.146), channel_id=1, source_target_pairs={{0,24},{4,28},{8,16},{12,20},{16,8},{20,12},{24,0},{28,4},{1,25},{... | collective-permute-start | bytes 442376 | tf_op jit(solution)/shard_map/ppermute | solution.py:57
  21.9 2.6 collective-permute-start.13
  25.4 5.1 %collective-permute-done.28 = bf16[96,768]{1,0:T(8,128)(2,1)S(1)} collective-permute-done((bf16[96,768]{1,0:T(8,128)(2,1)S(1)}, bf16[96,768]{1,0:T(8,128)(2,1)S(1)}, u32[]{:S(2)}, u32[]{:S(2)}) %collective-permute-start.28) | collective-permute-done | bytes 147488 | tf_op jit(solution)/shard_map/ppermute | solution.py:57
  30.5 2.9 collective-permute-start.15
  38.3 2.7 collective-permute-start.5
  41.0 8.0 %collective-permute-done.4 = bf16[288,192]{0,1:T(8,128)(2,1)S(1)} collective-permute-done((bf16[288,192]{0,1:T(8,128)(2,1)S(1)}, bf16[288,192]{0,1:T(8,128)(2,1)S(1)}, u32[]{:S(2)}, u32[]{:S(2)}) %collective-permute-start.4) | collective-permute-done | bytes 110624 | tf_op jit(solution)/shard_map/ppermute | solution.py:57
  53.5 13.3 %collective-permute-done.16 = bf16[4,96,192]{1,2,0:T(8,128)(2,1)S(1)} collective-permute-done((bf16[4,96,192]{1,2,0:T(8,128)(2,1)S(1)}, bf16[4,96,192]{1,2,0:T(8,128)(2,1)S(1)}, u32[]{:S(2)}, u32[]{:S(2)}) %collective-permute-start.16) | collective-permute-done | bytes 147488 | tf_op jit(solution)/shard_map/ppermute | solution.py:57
  76.1 3.0 collective-permute-done.18.c2
  83.3 2.4 pick.1
  87.7 2.4 collective-permute-start.8
  90.1 43.3 %collective-permute-done.8.w2 = bf16[576,192]{1,0:T(8,128)(2,1)S(1)} collective-permute-done((bf16[576,192]{1,0:T(8,128)(2,1)}, bf16[576,192]{1,0:T(8,128)(2,1)S(1)}, u32[]{:S(2)}, u32[]{:S(2)}) %collective-permute-start.8) | collective-permute-done | bytes 221216 | tf_op jit(solution)/shard_map/ppermute | solution.py:57
  133.4 39.2 %all-gather.1 = bf16[32,3,96]{2,1,0:T(4,128)(2,1)S(1)} all-gather(bf16[1,3,96]{2,1,0:T(4,128)(2,1)S(1)} %convert_bitcast_fusion.6), channel_id=2, replica_groups=mesh['dp'=8,'seq'=4] {'dp','seq'}, dimensions={0}, use_global_device_ids=true | all-gather | bytes 19008 | tf_op jit(solution)/shard_map/all_gather | solution.py:391
  175.6 21.8 %forward.1 = (bf16[9,2048,64]{2,1,0:T(8,128)(2,1)}, bf16[576,768]{1,0:T(8,128)(2,1)}, bf16[512,192]{1,0:T(8,128)(2,1)}, bf16[512,192]{1,0:T(8,128)(2,1)}, bf16[5...) custom-call(s32[2]{0:T(128)} %pad_add_fusion.place, bf16[512,768]{1,0:T(8,128)(2,1)} %bitcast.227, ...), custom_call_target="tpu_custom_call" | custom-call | flops 6000000000 | bytes 8128520 | tf_op jit(solution)/shard_map/forward/pallas_call | solution.py:82
  200.1 7.7 %collective-permute-done.11.a2 = bf16[512,192]{1,0:T(8,128)(2,1)S(1)} collective-permute-done((bf16[512,192]{1,0:T(8,128)(2,1)}, bf16[512,192]{1,0:T(8,128)(2,1)S(1)}, u32[]{:S(2)}, u32[]{:S(2)}) %collective-permute-start.11) | collective-permute-done | bytes 196640 | tf_op jit(solution)/shard_map/ppermute | solution.py:57
  209.2 7.0 %collective-permute-done.12.a3 = bf16[512,192]{1,0:T(8,128)(2,1)S(1)} collective-permute-done((bf16[512,192]{1,0:T(8,128)(2,1)}, bf16[512,192]{1,0:T(8,128)(2,1)S(1)}, u32[]{:S(2)}, u32[]{:S(2)}) %collective-permute-start.12) | collective-permute-done | bytes 196640 | tf_op jit(solution)/shard_map/ppermute | solution.py:57
  217.3 26.7 %middle.1 = (bf16[512,768]{1,0:T(8,128)(2,1)}, bf16[8,512,384]{2,1,0:T(8,128)(2,1)}, bf16[8,512,384]{2,1,0:T(8,128)(2,1)}, bf16[512,768]{1,0:T(8,128)(2,1)}, bf1...) custom-call(s32[2]{0:T(128)} %pad_add_fusion.place, ...), custom_call_target="tpu_custom_call" | custom-call | flops 12000000000 | bytes 24846344 | tf_op jit(solution)/shard_map/middle/pallas_call | solution.py:82
  245.9 16.7 %grads.1 = (bf16[2,8,192,384]{3,2,1,0:T(8,128)(2,1)}, bf16[2,8,192,384]{3,2,1,0:T(8,128)(2,1)}, bf16[2,8,96,768]{3,2,1,0:T(8,128)(2,1)}, bf16[2,8,96,768]{3,2,1,...) custom-call(s32[2]{0:T(128)} %pad_add_fusion.place, ...), custom_call_target="tpu_custom_call" | custom-call | flops 6000000000 | bytes 20054024 | tf_op jit(solution)/shard_map/grads/pallas_call | solution.py:82
  264.0 32.5 %backward.1 = (bf16[512,768]{1,0:T(8,128)(2,1)}, bf16[512,768]{1,0:T(8,128)(2,1)}, bf16[512,768]{1,0:T(8,128)(2,1)}, bf16[512,768]{1,0:T(8,128)(2,1)}, bf16[576,...) custom-call(s32[2]{0:T(128)} %pad_add_fusion.place, ...), custom_call_target="tpu_custom_call" | custom-call | flops 12000000000 | bytes 12069896 | tf_op jit(solution)/shard_map/backward/pallas_call | solution.py:82
  300.7 43.9 %psum.7 = f32[12,768]{1,0:T(8,128)S(1)} all-reduce(f32[12,768]{1,0:T(8,128)S(1)} %concatenate.3), channel_id=1, replica_groups=mesh['dp'=8,'seq'=4] {'dp','seq'}, use_global_device_ids=true, to_apply=%region_0.0 | all-reduce | flops 9216 | bytes 73728 | tf_op jit(solution)/shard_map/psum | solution.py:523
  345.9 2.4 arrange.1
  356.2 10.6 %collective-permute-done.43 = bf16[4,288,192]{1,2,0:T(8,128)(2,1)S(1)} collective-permute-done((bf16[4,288,192]{1,2,0:T(8,128)(2,1)}, bf16[4,288,192]{1,2,0:T(8,128)(2,1)S(1)}, u32[]{:S(2)}, u32[]{:S(2)}) %collective-permute-start.43) | collective-permute-done | bytes 442400 | tf_op jit(solution)/shard_map/ppermute | solution.py:57
  367.1 2.4 collective-permute-start.46
  377.4 5.7 %collective-permute-done.45 = bf16[288,192]{0,1:T(8,128)(2,1)S(1)} collective-permute-done((bf16[288,192]{0,1:T(8,128)(2,1)S(1)}, bf16[288,192]{0,1:T(8,128)(2,1)S(1)}, u32[]{:S(2)}, u32[]{:S(2)}) %collective-permute-start.45) | collective-permute-done | bytes 110624 | tf_op jit(solution)/shard_map/ppermute | solution.py:57
  394.5 2.4 collective-permute-start.52
  396.9 19.3 %collective-permute-done.54 = bf16[8,192,384]{2,1,0:T(8,128)(2,1)S(1)} collective-permute-done((bf16[8,192,384]{2,1,0:T(8,128)(2,1)S(1)}, bf16[8,192,384]{2,1,0:T(8,128)(2,1)S(1)}, u32[]{:S(2)}, u32[]{:S(2)}) %collective-permute-start.54) | collective-permute-done | bytes 1179680 | tf_op jit(solution)/shard_map/ppermute | solution.py:57
  424.7 8.4 %collective-permute-done.39.other = bf16[512,768]{1,0:T(8,128)(2,1)S(1)} collective-permute-done((bf16[512,768]{1,0:T(8,128)(2,1)S(1)}, bf16[512,768]{1,0:T(8,128)(2,1)S(1)}, u32[]{:S(2)}, u32[]{:S(2)}) %collective-permute-start.39) | collective-permute-done | bytes 786464 | tf_op jit(solution)/shard_map/ppermute | solution.py:57
  434.0 4.1 last.1
  439.4 2.4 collective-permute-start.58
  449.0 11.9 %collective-permute-done.57 = bf16[192,384]{1,0:T(8,128)(2,1)S(1)} collective-permute-done((bf16[192,384]{1,0:T(8,128)(2,1)S(1)}, bf16[192,384]{1,0:T(8,128)(2,1)S(1)}, u32[]{:S(2)}, u32[]{:S(2)}) %collective-permute-start.57) | collective-permute-done | bytes 147488 | tf_op jit(solution)/shard_map/ppermute | solution.py:57
  462.0 3.0 collective-permute-done.63
  (254 shorter events, 97.3 us)
Async XLA Ops:
  8.4 22.1 %collective-permute-start.28 = (bf16[96,768]{1,0:T(8,128)(2,1)S(1)}, bf16[96,768]{1,0:T(8,128)(2,1)S(1)}, u32[]{:S(2)}, u32[]{:S(2)}) collective-permute-start(bf16[96,768]{1,0:T(8,128)(2,1)S(1)} %get-tuple-element.146), channel_id=1, source_target_pairs={{0,16},{4,20},{8,24},{12,28},{16,0},{20,4},{24,8},{28,12},{1,17},{... | collective-permute-start | bytes 442376 | tf_op jit(solution)/shard_map/ppermute | solution.py:57
  10.4 23.1 %collective-permute-start.27 = (bf16[96,768]{1,0:T(8,128)(2,1)S(1)}, bf16[96,768]{1,0:T(8,128)(2,1)S(1)}, u32[]{:S(2)}, u32[]{:S(2)}) collective-permute-start(bf16[96,768]{1,0:T(8,128)(2,1)S(1)} %get-tuple-element.146), channel_id=1, source_target_pairs={{0,8},{4,12},{8,0},{12,4},{16,24},{20,28},{24,16},{28,20},{1,9},{5... | collective-permute-start | bytes 442376 | tf_op jit(solution)/shard_map/ppermute | solution.py:57
  14.5 20.5 %collective-permute-start.29 = (bf16[96,768]{1,0:T(8,128)(2,1)S(1)}, bf16[96,768]{1,0:T(8,128)(2,1)S(1)}, u32[]{:S(2)}, u32[]{:S(2)}) collective-permute-start(bf16[96,768]{1,0:T(8,128)(2,1)S(1)} %get-tuple-element.146), channel_id=1, source_target_pairs={{0,24},{4,28},{8,16},{12,20},{16,8},{20,12},{24,0},{28,4},{1,25},{... | collective-permute-start | bytes 442376 | tf_op jit(solution)/shard_map/ppermute | solution.py:57
  33.4 35.9 %collective-permute-start.23 = (bf16[4,192,384]{2,1,0:T(8,128)(2,1)}, bf16[4,192,384]{2,1,0:T(8,128)(2,1)}, u32[]{:S(2)}, u32[]{:S(2)}) collective-permute-start(bf16[4,192,384]{2,1,0:T(8,128)(2,1)} %get-tuple-element.140), channel_id=1, source_target_pairs={{0,4},{4,0},{8,12},{12,8},{16,20},{20,16},{24,28},{28,24},{1,5},{5... | collective-permute-start | bytes 1769480 | tf_op jit(solution)/shard_map/ppermute | solution.py:57
  35.9 35.9 %collective-permute-start.30 = (bf16[4,96,768]{2,1,0:T(8,128)(2,1)}, bf16[4,96,768]{2,1,0:T(8,128)(2,1)}, u32[]{:S(2)}, u32[]{:S(2)}) collective-permute-start(bf16[4,96,768]{2,1,0:T(8,128)(2,1)} %get-tuple-element.138), channel_id=1, source_target_pairs={{0,4},{4,0},{8,12},{12,8},{16,20},{20,16},{24,28},{28,24},{1,5},{5... | collective-permute-start | bytes 1769480 | tf_op jit(solution)/shard_map/ppermute | solution.py:57
  49.9 36.4 %collective-permute-start.1 = (bf16[512,768]{1,0:T(8,128)(2,1)S(1)}, bf16[512,768]{1,0:T(8,128)(2,1)}, u32[]{:S(2)}, u32[]{:S(2)}) collective-permute-start(bf16[512,768]{1,0:T(8,128)(2,1)S(1)} %bitcast.231), channel_id=1, source_target_pairs={{0,2},{1,3},{2,0},{3,1},{4,6},{5,7},{6,4},{7,5},{8,10},{9,11},{10,... | collective-permute-start | bytes 2359304 | tf_op jit(solution)/shard_map/ppermute | solution.py:57
  52.4 28.2 %collective-permute-start.6 = (bf16[4,288,192]{1,2,0:T(8,128)(2,1)}, bf16[4,288,192]{1,2,0:T(8,128)(2,1)}, u32[]{:S(2)}, u32[]{:S(2)}) collective-permute-start(bf16[4,288,192]{1,2,0:T(8,128)(2,1)} %get-tuple-element.142), channel_id=1, source_target_pairs={{0,4},{4,0},{8,12},{12,8},{16,20},{20,16},{24,28},{28,24},{1,5},{5... | collective-permute-start | bytes 1327112 | tf_op jit(solution)/shard_map/ppermute | solution.py:57
  74.0 99.3 %collective-permute-start.32 = (bf16[8,96,768]{2,1,0:T(8,128)(2,1)}, bf16[8,96,768]{2,1,0:T(8,128)(2,1)}, u32[]{:S(2)}, u32[]{:S(2)}) collective-permute-start(bf16[8,96,768]{2,1,0:T(8,128)(2,1)} %bitcast.37.p0), channel_id=1, source_target_pairs={{0,2},{1,3},{2,0},{3,1},{4,6},{5,7},{6,4},{7,5},{8,10},{9,11},{10,... | collective-permute-start | bytes 3538952 | tf_op jit(solution)/shard_map/ppermute | solution.py:57
  74.6 99.1 %collective-permute-start.25 = (bf16[8,192,384]{2,1,0:T(8,128)(2,1)}, bf16[8,192,384]{2,1,0:T(8,128)(2,1)}, u32[]{:S(2)}, u32[]{:S(2)}) collective-permute-start(bf16[8,192,384]{2,1,0:T(8,128)(2,1)} %bitcast.29.f0), channel_id=1, source_target_pairs={{0,2},{1,3},{2,0},{3,1},{4,6},{5,7},{6,4},{7,5},{8,10},{9,11},{10,... | collective-permute-start | bytes 3538952 | tf_op jit(solution)/shard_map/ppermute | solution.py:57
  80.5 92.6 %collective-permute-start = (bf16[512,768]{1,0:T(8,128)(2,1)S(1)}, bf16[512,768]{1,0:T(8,128)(2,1)}, u32[]{:S(2)}, u32[]{:S(2)}) collective-permute-start(bf16[512,768]{1,0:T(8,128)(2,1)S(1)} %bitcast.232), channel_id=1, source_target_pairs={{0,1},{1,0},{2,3},{3,2},{4,5},{5,4},{6,7},{7,6},{8,9},{9,8},{10,11... | collective-permute-start | bytes 2359304 | tf_op jit(solution)/shard_map/ppermute | solution.py:57
  86.3 89.0 %collective-permute-start.2 = (bf16[512,768]{1,0:T(8,128)(2,1)}, bf16[512,768]{1,0:T(8,128)(2,1)}, u32[]{:S(2)}, u32[]{:S(2)}) collective-permute-start(bf16[512,768]{1,0:T(8,128)(2,1)} %collective-permute-done.1.x2), channel_id=1, source_target_pairs={{0,1},{1,0},{2,3},{3,2},{4,5},{5,4},{6,7},{7,6},{8,9},{9,8},{10,11... | collective-permute-start | bytes 2359304 | tf_op jit(solution)/shard_map/ppermute | solution.py:57
  87.7 45.7 %collective-permute-start.8 = (bf16[576,192]{1,0:T(8,128)(2,1)}, bf16[576,192]{1,0:T(8,128)(2,1)S(1)}, u32[]{:S(2)}, u32[]{:S(2)}) collective-permute-start(bf16[576,192]{1,0:T(8,128)(2,1)} %get-tuple-element.64), channel_id=1, source_target_pairs={{0,2},{1,3},{2,0},{3,1},{4,6},{5,7},{6,4},{7,5},{8,10},{9,11},{10,... | collective-permute-start | bytes 663560 | tf_op jit(solution)/shard_map/ppermute | solution.py:57
  133.4 39.3 %collective-permute-start.9 = (bf16[576,192]{1,0:T(8,128)(2,1)}, bf16[576,192]{1,0:T(8,128)(2,1)S(1)}, u32[]{:S(2)}, u32[]{:S(2)}) collective-permute-start(bf16[576,192]{1,0:T(8,128)(2,1)} %get-tuple-element.65), channel_id=1, source_target_pairs={{0,3},{1,2},{2,1},{3,0},{4,7},{5,6},{6,5},{7,4},{8,11},{9,10},{10,... | collective-permute-start | bytes 663560 | tf_op jit(solution)/shard_map/ppermute | solution.py:57
  172.8 43.4 %collective-permute-start.31 = (bf16[8,96,768]{2,1,0:T(8,128)(2,1)}, bf16[8,96,768]{2,1,0:T(8,128)(2,1)S(1)}, u32[]{:S(2)}, u32[]{:S(2)}) collective-permute-start(bf16[8,96,768]{2,1,0:T(8,128)(2,1)} %bitcast.37.p0), channel_id=1, source_target_pairs={{0,1},{1,0},{2,3},{3,2},{4,5},{5,4},{6,7},{7,6},{8,9},{9,8},{10,11... | collective-permute-start | bytes 3538952 | tf_op jit(solution)/shard_map/ppermute | solution.py:57
  173.2 43.0 %collective-permute-start.24 = (bf16[8,192,384]{2,1,0:T(8,128)(2,1)}, bf16[8,192,384]{2,1,0:T(8,128)(2,1)}, u32[]{:S(2)}, u32[]{:S(2)}) collective-permute-start(bf16[8,192,384]{2,1,0:T(8,128)(2,1)} %bitcast.29.f0), channel_id=1, source_target_pairs={{0,1},{1,0},{2,3},{3,2},{4,5},{5,4},{6,7},{7,6},{8,9},{9,8},{10,11... | collective-permute-start | bytes 3538952 | tf_op jit(solution)/shard_map/ppermute | solution.py:57
  173.4 42.8 %collective-permute-start.33 = (bf16[8,96,768]{2,1,0:T(8,128)(2,1)}, bf16[8,96,768]{2,1,0:T(8,128)(2,1)}, u32[]{:S(2)}, u32[]{:S(2)}) collective-permute-start(bf16[8,96,768]{2,1,0:T(8,128)(2,1)} %collective-permute-done.32.p2), channel_id=1, source_target_pairs={{0,1},{1,0},{2,3},{3,2},{4,5},{5,4},{6,7},{7,6},{8,9},{9,8},{10,11... | collective-permute-start | bytes 3538952 | tf_op jit(solution)/shard_map/ppermute | solution.py:57
  173.7 42.5 %collective-permute-start.26 = (bf16[8,192,384]{2,1,0:T(8,128)(2,1)}, bf16[8,192,384]{2,1,0:T(8,128)(2,1)}, u32[]{:S(2)}, u32[]{:S(2)}) collective-permute-start(bf16[8,192,384]{2,1,0:T(8,128)(2,1)} %collective-permute-done.25.f2), channel_id=1, source_target_pairs={{0,1},{1,0},{2,3},{3,2},{4,5},{5,4},{6,7},{7,6},{8,9},{9,8},{10,11... | collective-permute-start | bytes 3538952 | tf_op jit(solution)/shard_map/ppermute | solution.py:57
  175.2 22.1 %collective-permute-start.19 = (bf16[8,96,192]{2,1,0:T(8,128)(2,1)}, bf16[8,96,192]{2,1,0:T(8,128)(2,1)S(1)}, u32[]{:S(2)}, u32[]{:S(2)}) collective-permute-start(bf16[8,96,192]{2,1,0:T(8,128)(2,1)} %copy-done.31), channel_id=1, source_target_pairs={{0,1},{1,0},{2,3},{3,2},{4,5},{5,4},{6,7},{7,6},{8,9},{9,8},{10,11... | collective-permute-start | bytes 884744 | tf_op jit(solution)/shard_map/ppermute | solution.py:57
  262.7 123.0 %collective-permute-start.53 = (bf16[2,8,192,384]{3,2,1,0:T(8,128)(2,1)}, bf16[2,8,192,384]{3,2,1,0:T(8,128)(2,1)}, u32[]{:S(2)}, u32[]{:S(2)}) collective-permute-start(bf16[2,8,192,384]{3,2,1,0:T(8,128)(2,1)} %get-tuple-element.95), channel_id=1, source_target_pairs={{0,1},{1,0},{2,3},{3,2},{4,5},{5,4},{6,7},{7,6},{8,9},{9,8},{10,11... | collective-permute-start | bytes 7077896 | tf_op jit(solution)/shard_map/ppermute | solution.py:57
  296.5 48.1 %collective-permute-start.40 = (bf16[576,192]{1,0:T(8,128)(2,1)}, bf16[576,192]{1,0:T(8,128)(2,1)S(1)}, u32[]{:S(2)}, u32[]{:S(2)}) collective-permute-start(bf16[576,192]{1,0:T(8,128)(2,1)} %get-tuple-element.84), channel_id=1, source_target_pairs={{0,1},{1,0},{2,3},{3,2},{4,5},{5,4},{6,7},{7,6},{8,9},{9,8},{10,11... | collective-permute-start | bytes 663560 | tf_op jit(solution)/shard_map/ppermute | solution.py:57
  296.7 48.0 %collective-permute-start.41 = (bf16[576,192]{1,0:T(8,128)(2,1)}, bf16[576,192]{1,0:T(8,128)(2,1)S(1)}, u32[]{:S(2)}, u32[]{:S(2)}) collective-permute-start(bf16[576,192]{1,0:T(8,128)(2,1)} %get-tuple-element.85), channel_id=1, source_target_pairs={{0,2},{1,3},{2,0},{3,1},{4,6},{5,7},{6,4},{7,5},{8,10},{9,11},{10,... | collective-permute-start | bytes 663560 | tf_op jit(solution)/shard_map/ppermute | solution.py:57
  297.7 47.5 %collective-permute-start.42 = (bf16[576,192]{1,0:T(8,128)(2,1)}, bf16[576,192]{1,0:T(8,128)(2,1)S(1)}, u32[]{:S(2)}, u32[]{:S(2)}) collective-permute-start(bf16[576,192]{1,0:T(8,128)(2,1)} %get-tuple-element.86), channel_id=1, source_target_pairs={{0,3},{1,2},{2,1},{3,0},{4,7},{5,6},{6,5},{7,4},{8,11},{9,10},{10,... | collective-permute-start | bytes 663560 | tf_op jit(solution)/shard_map/ppermute | solution.py:57
  298.5 55.6 %collective-permute-start.47 = (bf16[2,8,96,192]{3,2,1,0:T(8,128)(2,1)}, bf16[2,8,96,192]{3,2,1,0:T(8,128)(2,1)}, u32[]{:S(2)}, u32[]{:S(2)}) collective-permute-start(bf16[2,8,96,192]{3,2,1,0:T(8,128)(2,1)} %get-tuple-element.93), channel_id=1, source_target_pairs={{0,1},{1,0},{2,3},{3,2},{4,5},{5,4},{6,7},{7,6},{8,9},{9,8},{10,11... | collective-permute-start | bytes 1769480 | tf_op jit(solution)/shard_map/ppermute | solution.py:57
  344.6 46.3 %collective-permute-start.59 = (bf16[2,8,96,768]{3,2,1,0:T(8,128)(2,1)}, bf16[2,8,96,768]{3,2,1,0:T(8,128)(2,1)}, u32[]{:S(2)}, u32[]{:S(2)}) collective-permute-start(bf16[2,8,96,768]{3,2,1,0:T(8,128)(2,1)} %get-tuple-element.97), channel_id=1, source_target_pairs={{0,1},{1,0},{2,3},{3,2},{4,5},{5,4},{6,7},{7,6},{8,9},{9,8},{10,11... | collective-permute-start | bytes 7077896 | tf_op jit(solution)/shard_map/ppermute | solution.py:57
  344.7 43.7 %collective-permute-start.38 = (bf16[512,768]{1,0:T(8,128)(2,1)}, bf16[512,768]{1,0:T(8,128)(2,1)}, u32[]{:S(2)}, u32[]{:S(2)}) collective-permute-start(bf16[512,768]{1,0:T(8,128)(2,1)} %get-tuple-element.82), channel_id=1, source_target_pairs={{0,1},{1,0},{2,3},{3,2},{4,5},{5,4},{6,7},{7,6},{8,9},{9,8},{10,11... | collective-permute-start | bytes 2359304 | tf_op jit(solution)/shard_map/ppermute | solution.py:57
  387.3 29.0 %collective-permute-start.54 = (bf16[8,192,384]{2,1,0:T(8,128)(2,1)S(1)}, bf16[8,192,384]{2,1,0:T(8,128)(2,1)S(1)}, u32[]{:S(2)}, u32[]{:S(2)}) collective-permute-start(bf16[8,192,384]{2,1,0:T(8,128)(2,1)S(1)} %fusion.3), channel_id=1, source_target_pairs={{0,2},{1,3},{2,0},{3,1},{4,6},{5,7},{6,4},{7,5},{8,10},{9,11},{10,... | collective-permute-start | bytes 3538952 | tf_op jit(solution)/shard_map/ppermute | solution.py:57
  389.9 43.2 %collective-permute-start.39 = (bf16[512,768]{1,0:T(8,128)(2,1)S(1)}, bf16[512,768]{1,0:T(8,128)(2,1)S(1)}, u32[]{:S(2)}, u32[]{:S(2)}) collective-permute-start(bf16[512,768]{1,0:T(8,128)(2,1)S(1)} %add_convert_fusion.4), channel_id=1, source_target_pairs={{0,2},{1,3},{2,0},{3,1},{4,6},{5,7},{6,4},{7,5},{8,10},{9,11},{10,... | collective-permute-start | bytes 2359304 | tf_op jit(solution)/shard_map/ppermute | solution.py:57
  392.6 26.5 %collective-permute-start.60 = (bf16[2,4,96,768]{3,2,1,0:T(8,128)(2,1)S(1)}, bf16[2,4,96,768]{3,2,1,0:T(8,128)(2,1)S(1)}, u32[]{:S(2)}, u32[]{:S(2)}) collective-permute-start(bf16[2,4,96,768]{3,2,1,0:T(8,128)(2,1)S(1)} %fusion.5), channel_id=1, source_target_pairs={{0,4},{4,0},{8,12},{12,8},{16,20},{20,16},{24,28},{28,24},{1,5},{5... | collective-permute-start | bytes 3538952 | tf_op jit(solution)/shard_map/ppermute | solution.py:57
  394.5 28.2 %collective-permute-start.50 = (bf16[96,192]{0,1:T(8,128)(2,1)S(1)}, bf16[96,192]{0,1:T(8,128)(2,1)S(1)}, u32[]{:S(2)}, u32[]{:S(2)}) collective-permute-start(bf16[96,192]{0,1:T(8,128)(2,1)S(1)} %get-tuple-element.149), channel_id=1, source_target_pairs={{0,8},{4,12},{8,0},{12,4},{16,24},{20,28},{24,16},{28,20},{1,9},{5... | collective-permute-start | bytes 110600 | tf_op jit(solution)/shard_map/ppermute | solution.py:57
  394.5 29.4 %collective-permute-start.52 = (bf16[96,192]{0,1:T(8,128)(2,1)S(1)}, bf16[96,192]{0,1:T(8,128)(2,1)S(1)}, u32[]{:S(2)}, u32[]{:S(2)}) collective-permute-start(bf16[96,192]{0,1:T(8,128)(2,1)S(1)} %get-tuple-element.150), channel_id=1, source_target_pairs={{0,24},{4,28},{8,16},{12,20},{16,8},{20,12},{24,0},{28,4},{1,25},{... | collective-permute-start | bytes 110600 | tf_op jit(solution)/shard_map/ppermute | solution.py:57
  422.7 21.2 %collective-permute-start.61 = (bf16[4,96,768]{2,1,0:T(8,128)(2,1)}, bf16[4,96,768]{2,1,0:T(8,128)(2,1)S(1)}, u32[]{:S(2)}, u32[]{:S(2)}) collective-permute-start(bf16[4,96,768]{2,1,0:T(8,128)(2,1)} %slice_bitcast_fusion.4), channel_id=1, source_target_pairs={{0,2},{1,3},{2,0},{3,1},{4,6},{5,7},{6,4},{7,5},{8,10},{9,11},{10,... | collective-permute-start | bytes 1769480 | tf_op jit(solution)/shard_map/ppermute | solution.py:57
  441.8 19.0 %collective-permute-start.57 = (bf16[192,384]{1,0:T(8,128)(2,1)S(1)}, bf16[192,384]{1,0:T(8,128)(2,1)S(1)}, u32[]{:S(2)}, u32[]{:S(2)}) collective-permute-start(bf16[192,384]{1,0:T(8,128)(2,1)S(1)} %get-tuple-element.133), channel_id=1, source_target_pairs={{0,16},{4,20},{8,24},{12,28},{16,0},{20,4},{24,8},{28,12},{1,17},{... | collective-permute-start | bytes 442376 | tf_op jit(solution)/shard_map/ppermute | solution.py:57
  (75 other events, 888.5 us)
